TPU v7x, 512 devices: a whole 4x4x16 slice. The times are simulated.
512 devices in a mesh: grp: 4 (over x_lo, core), dp: 32 (over z, x_hi), mp: 4 (over y).
Axes of the slice: x: 4 (x_hi: 2, x_lo: 2; x = x_hi * 2 + x_lo), y: 4, z: 16, core: 2. Of those that a mesh axis runs over, the one named last changes fastest.
Arguments:
- neighbours: bfloat16 [512, 256, 896], P(('grp', 'dp')), may hold values from -6 to 6
- counts: int32 [512], P(('grp', 'dp')), may hold values from 0 to 2
- owner: int32 [512], P(('grp', 'dp')), may hold values from 0 to 511, as said below
- norm_gain: float32 [896], replicated, may hold values from 0.1 to 1.9
- w_in: bfloat16 [896, 3584], P('dp', 'mp'), may hold values from -0.1875 to 0.1875
- w_out: bfloat16 [3584, 896], P('mp', 'dp'), may hold values from -0.09375 to 0.09375
- w_key: bfloat16 [896, 4096], P('dp', 'mp'), may hold values from -0.1875 to 0.1875
- w_value: bfloat16 [896, 4096], P('dp', 'mp'), may hold values from -0.1875 to 0.1875
- queries: bfloat16 [32768, 4096], P(('grp', 'dp'), 'mp'), may hold values from -150 to 150
Outputs:
- attended: bfloat16 [32768, 4096], P(('grp', 'dp'), 'mp')
Inputs may be any that keep to these rules, and one draw needn't show every extreme that they name: owner is a permutation of the 512 query blocks. Span c stands on device c // 4 of grp+dp (index grp * 32 + dp); block owner[c] lies on device owner[c] // 4, which has the same dp index. Each device keeps 2 of its spans (their blocks lie on the device itself) and sends the other 2 to one other device along grp.
All inputs are finite; a program needn't handle non-finite values.
Results may differ from a plain program's by a relative error of at most 0.02.
Values may be sent and summed in bfloat16 or wider, within the bound.
A program may use at most 64 MiB of HBM per device.

v0:
```python
import jax
import jax.numpy as jnp
from jax import lax
from jax.sharding import PartitionSpec as P

HEAD = 128
NLEN = 128


def place_rows(received, meta, span_count):
    targets = jnp.arange(span_count, dtype=jnp.int32)[:, None]
    picker = meta[:, 0][None, :] == targets
    placed = jnp.einsum(
        "jb,btc->jtc", picker.astype(jnp.bfloat16), received, preferred_element_type=jnp.float32
    ).astype(jnp.bfloat16)
    live_counts = jnp.sum(jnp.where(picker, meta[:, 1][None, :], 0), axis=1).astype(jnp.int32)
    return (placed, live_counts)


def route_table(dest_grp, dest_slot, valid, extra, group_count, capacity):
    entries = dest_grp.shape[0]
    order = jnp.arange(entries, dtype=jnp.int32)
    earlier = (
        valid[None, :]
        & (dest_grp[None, :] == dest_grp[:, None])
        & (order[None, :] < order[:, None])
    )
    rank = jnp.sum(earlier.astype(jnp.int32), axis=1)
    bucket = jnp.where(valid, dest_grp * capacity + rank, -1)
    picker = bucket[None, :] == jnp.arange(group_count * capacity, dtype=jnp.int32)[:, None]
    slot_sent = jnp.sum(jnp.where(picker, dest_slot[None, :] + 1, 0), axis=1) - 1
    extra_sent = jnp.sum(jnp.where(picker, extra[None, :], 0), axis=1)
    meta = jnp.stack([slot_sent, extra_sent], axis=1)
    return (picker, meta)


def bucket_rows(rows, owner, extra, group_count, dp_count):
    span_count = owner.shape[0]
    dest_grp = owner // span_count // dp_count
    dest_slot = owner % span_count
    valid = jnp.ones((span_count,), dtype=bool)
    picker, meta = route_table(dest_grp, dest_slot, valid, extra, group_count, span_count // 2)
    packed = jnp.einsum(
        "bj,jtc->btc", picker.astype(jnp.bfloat16), rows, preferred_element_type=jnp.float32
    ).astype(jnp.bfloat16)
    return (packed, meta)


def attend_local(query_blocks, keys, values, live_counts):
    key_len = keys.shape[1]
    scores = jnp.einsum(
        "cqhd,ckhd->chqk", query_blocks, keys, preferred_element_type=jnp.float32
    ) * HEAD ** (-0.5)
    position = jnp.arange(key_len, dtype=jnp.int32) // NLEN
    live = (position[None, :] < live_counts[:, None])[:, None, None, :]
    masked = jnp.where(live, scores, -1e30)
    top = jnp.maximum(jnp.max(masked, axis=-1), 0.0)
    probs = jnp.where(live, jnp.exp(masked - top[..., None]), 0.0)
    denom = jnp.sum(probs, axis=-1) + jnp.exp(-top)
    weights = probs.astype(jnp.bfloat16)
    mixed = jnp.einsum("chqk,ckhd->cqhd", weights, values, preferred_element_type=jnp.float32)
    mixed = mixed / jnp.transpose(denom, (0, 2, 1))[..., None]
    span_count, span_len = (mixed.shape[0], mixed.shape[1])
    return mixed.astype(jnp.bfloat16).reshape(span_count, span_len, -1)


def on_device(neighbours, counts, owner, norm_gain, w_in, w_out, w_key, w_value, queries):
    span_count, key_len, enc_width = neighbours.shape
    group_count = lax.axis_size("grp")
    dp_count = lax.axis_size("dp")
    local_width = queries.shape[1]
    query_rows = queries.reshape(span_count, -1, local_width)
    flat = neighbours.astype(jnp.float32).reshape(-1, enc_width)
    meansq = jnp.mean(flat * flat, axis=-1, keepdims=True)
    normed = (flat * lax.rsqrt(meansq + 1e-06) * norm_gain).astype(jnp.bfloat16)
    columns = normed
    pre = jnp.dot(
        columns, lax.all_gather(w_in, "dp", axis=0, tiled=True), preferred_element_type=jnp.float32
    )
    hidden = jax.nn.gelu(pre, approximate=False).astype(jnp.bfloat16)
    partial_out = jnp.dot(
        hidden, lax.all_gather(w_out, "dp", axis=1, tiled=True), preferred_element_type=jnp.float32
    )
    total = lax.psum(partial_out, "mp")
    states = (flat + total).astype(jnp.bfloat16).reshape(span_count, key_len, enc_width)
    packed, meta = bucket_rows(states, owner, counts, group_count, dp_count)
    received, received_meta = (
        lax.all_to_all(packed, "grp", split_axis=0, concat_axis=0, tiled=True),
        lax.all_to_all(meta, "grp", split_axis=0, concat_axis=0, tiled=True),
    )
    served, live_counts = place_rows(received, received_meta, span_count)
    served_flat = served.reshape(-1, enc_width)
    columns = served_flat
    key_total = jnp.dot(
        columns, lax.all_gather(w_key, "dp", axis=0, tiled=True), preferred_element_type=jnp.float32
    )
    value_total = jnp.dot(
        columns,
        lax.all_gather(w_value, "dp", axis=0, tiled=True),
        preferred_element_type=jnp.float32,
    )
    heads = w_key.shape[1] // HEAD
    keys = key_total.astype(jnp.bfloat16).reshape(span_count, key_len, heads, HEAD)
    values = value_total.astype(jnp.bfloat16).reshape(span_count, key_len, heads, HEAD)
    query_blocks = query_rows.reshape(span_count, -1, heads, HEAD)
    mixed = attend_local(query_blocks, keys, values, live_counts)
    return mixed.reshape(queries.shape[0], queries.shape[1])


def solution(mesh):
    placed = (
        P(("grp", "dp"), None, None),
        P(("grp", "dp")),
        P(("grp", "dp")),
        P(),
        P("dp", "mp"),
        P("mp", "dp"),
        P("dp", "mp"),
        P("dp", "mp"),
        P(("grp", "dp"), "mp"),
    )
    return jax.shard_map(
        on_device, mesh=mesh, in_specs=placed, out_specs=P(("grp", "dp"), "mp"), check_vma=False
    )
```

profile of v0, /device:TPU:8, one launch (start us, length us, event | category | flops | bytes accessed | tf_op | source)
XLA Modules:
  0.0 746.3 jit_solution(8559613204974902349)
XLA Ops:
  8.1 1.9 fusion.3
  10.0 2.0 fusion.5
  12.0 150.9 %all-gather.11.cloned.1.call-done = bf16[32,28,896]{2,1,0:T(8,128)(2,1)} async-done(((bf16[1,28,896]{2,1,0:T(8,128)(2,1)}), bf16[32,28,896]{2,1,0:T(8,128)(2,1)}) %all-gather.11.cloned.1.call-update) | async-done | bytes 1605648 | tf_op jit(solution)/shard_map/all_gather | solution.py:82
  162.9 2.4 reshape.107
  165.3 143.2 %all-gather.9.cloned.1.call-done = bf16[32,28,896]{2,1,0:T(8,128)(2,1)} async-done(((bf16[1,28,896]{2,1,0:T(8,128)(2,1)}), bf16[32,28,896]{2,1,0:T(8,128)(2,1)}) %all-gather.9.cloned.1.call-update) | async-done | bytes 1605648 | tf_op jit(solution)/shard_map/all_gather | solution.py:78
  308.5 3.5 reshape.105
  312.0 14.2 %fusion.23 = f32[1024,896]{1,0:T(8,128)} fusion(bf16[896,896]{1,0:T(8,128)(2,1)S(1)} %reshape.107, bf16[1024,896]{1,0:T(8,128)(2,1)S(1)} %fusion.5, bf16[896,896]{1,0:T(8,128)(2,1)} %reshape.105), kind=kOutput, calls=%fused_computation.41 | convolution fusion | flops 3347972096 | bytes 8716288 | tf_op jit(solution)/shard_map/dot_general | solution.py:81
  328.6 3.4 all-to-all-start
  332.0 87.4 %all-reduce.2.cloned.1.call-done = f32[1024,896]{1,0:T(8,128)} async-done(((f32[1024,896]{1,0:T(8,128)}), f32[1024,896]{1,0:T(8,128)}) %all-reduce.2.cloned.1.call-update) | async-done | bytes 3670032 | tf_op jit(solution)/shard_map/psum | solution.py:84
  419.4 2.4 fusion.6
  421.8 2.8 convolution_convert_fusion
  424.6 2.4 copy.31
  427.0 4.9 all-to-all-start.1
  432.3 141.0 %all-gather.13.cloned.1.call-done = bf16[32,28,1024]{2,1,0:T(8,128)(2,1)} async-done(((bf16[1,28,1024]{2,1,0:T(8,128)(2,1)}), bf16[32,28,1024]{2,1,0:T(8,128)(2,1)}) %all-gather.13.cloned.1.call-update) | async-done | bytes 1835024 | tf_op jit(solution)/shard_map/all_gather | solution.py:99
  573.3 2.5 reshape.109
  575.8 144.5 %all-gather.15.cloned.1.call-done = bf16[32,28,1024]{2,1,0:T(8,128)(2,1)} async-done(((bf16[1,28,1024]{2,1,0:T(8,128)(2,1)}), bf16[32,28,1024]{2,1,0:T(8,128)(2,1)}) %all-gather.15.cloned.1.call-update) | async-done | bytes 1835024 | tf_op jit(solution)/shard_map/all_gather | solution.py:95
  720.3 3.7 reshape.111
  724.1 4.5 fusion.25
  728.8 2.4 convert_bitcast_fusion.1
  732.6 2.3 convert_bitcast_fusion
  735.6 0.9 bitcast_reduce_fusion
  736.5 0.9 fusion.28
  737.5 1.0 fusion.36
  738.8 0.9 copy.66
  (46 shorter events, 6.8 us)
Async XLA Ops:
  6.5 156.4 %all-gather.11.cloned.1.call-start = ((), (), s32[]{:S(2)}) async-start(), calls=%async_computation.4 | async-start | bytes 1892352 | tf_op jit(solution)/shard_map/all_gather | solution.py:82
  7.3 301.2 %all-gather.9.cloned.1.call-start = ((), (), s32[]{:S(2)}) async-start(), calls=%async_computation.3 | async-start | bytes 1892352 | tf_op jit(solution)/shard_map/all_gather | solution.py:78
  8.0 411.4 %all-reduce.2.cloned.1.call-start = ((), (), s32[]{:S(2)}) async-start(), calls=%async_computation.2 | async-start | bytes 7340032 | tf_op jit(solution)/shard_map/psum | solution.py:84
  326.3 1.2 copy-start.4
  326.3 1.4 copy-start.3
  326.3 93.1 %copy-start = (bf16[4,256,896]{2,1,0:T(8,128)(2,1)S(1)}, bf16[4,256,896]{2,1,0:T(8,128)(2,1)}, u32[]{:S(2)}) copy-start(bf16[4,256,896]{2,1,0:T(8,128)(2,1)} %param.9) | copy-start | bytes 5505028
  326.3 247.1 %all-gather.13.cloned.1.call-start = ((), (), s32[]{:S(2)}) async-start(), calls=%async_computation.5 | async-start | bytes 2162688 | tf_op jit(solution)/shard_map/all_gather | solution.py:99
  326.9 393.5 %all-gather.15.cloned.1.call-start = ((), (), s32[]{:S(2)}) async-start(), calls=%async_computation.6 | async-start | bytes 2162688 | tf_op jit(solution)/shard_map/all_gather | solution.py:95
  328.6 98.5 %all-to-all-start = ((s32[4,2,2]{1,2,0:T(2,128)}), s32[4,2,2]{1,2,0:T(2,128)S(1)}, u32[]{:S(2)}, u32[]{:S(2)}) async-start(s32[4,2,2]{1,2,0:T(2,128)} %copy.28), calls=%async_computation | async-start | bytes 8192 | tf_op jit(solution)/shard_map/all_to_all | solution.py:89
  427.0 4.9 copy-start.2
  427.0 297.0 %all-to-all-start.1 = ((bf16[8,256,896]{2,1,0:T(8,128)(2,1)}), bf16[8,256,896]{2,1,0:T(8,128)(2,1)}, u32[]{:S(2)}, u32[]{:S(2)}) async-start(bf16[8,256,896]{2,1,0:T(8,128)(2,1)} %copy.31), calls=%async_computation.1 | async-start | bytes 7340032 | tf_op jit(solution)/shard_map/all_to_all | solution.py:88
  731.1 1.5 copy-start.1
Sparse Core Ops, SparseCore 0:
  10.4 152.4 all-gather.10
  166.0 142.4 all-gather.8
  326.4 92.9 all-reduce.1
  422.3 150.9 all-gather.12
  576.3 144.0 all-gather.14
where the time goes:
time: 747 us; the launch traced here: 746 us
  waiting for transfers between devices  669 us (90%)
  matrix products  28.1 us (4%)
  local copies, waits for them, and re-layouts  19.1 us (3%)
  between operations  13.4 us (2%)
  starting transfers between devices  8.46 us (1%)
  other arithmetic  7.76 us (1%)
    all_gather x1, waiting for transfers between devices, on_device(): lax.all_gather(w_out, 'dp', axis=1, tiled=True)  151 us
    all_gather x1, waiting for transfers between devices, on_device(): lax.all_gather(w_key, 'dp', axis=0, tiled=True)  145 us
    all_gather x1, waiting for transfers between devices, on_device(): lax.all_gather(w_in, 'dp', axis=0, tiled=True)  143 us
    all_gather x1, waiting for transfers between devices, on_device(): lax.all_gather(w_value, 'dp', axis=0, tiled=True)  141 us
    psum x1, waiting for transfers between devices, on_device(): total = lax.psum(partial_out, 'mp')  87.4 us
    unnamed x19, local copies, waits for them, and re-layouts  15.3 us
  transfers between devices with their start and end apart: 7, of which 5 were waited for; matrix products, arithmetic and copies ran while one was open for 3% of the time, Pallas kernels for 0%

commit v1 on v0

--- a/solution.py
+++ b/solution.py
@@ -79,7 +79,11 @@
     )
     hidden = jax.nn.gelu(pre, approximate=False).astype(jnp.bfloat16)
     partial_out = jnp.dot(
-        hidden, lax.all_gather(w_out, "dp", axis=1, tiled=True), preferred_element_type=jnp.float32
+        hidden,
+        jnp.concatenate(
+            lax.all_to_all(jnp.stack([w_out] * lax.axis_size("dp")), "dp", 0, 0), axis=1
+        ),
+        preferred_element_type=jnp.float32,
     )
     total = lax.psum(partial_out, "mp")
     states = (flat + total).astype(jnp.bfloat16).reshape(span_count, key_len, enc_width)

time: 747 us -> 634 us (0.85)
  waiting for transfers between devices: 669 us -> 537 us
  starting transfers between devices: 8.46 us -> 26.5 us
    all_gather x1 -> x0, waiting for transfers between devices: 151 us -> none  [on_device(): lax.all_gather(w_out, 'dp', axis=1, tiled=True)]
    all_gather x1, waiting for transfers between devices: 143 us -> 163 us  [on_device(): lax.all_gather(w_in, 'dp', axis=0, tiled=True)]
    all_to_all x0 -> x1, starting transfers between devices: none -> 18.1 us  [on_device(): lax.all_to_all(jnp.stack([w_out] * lax.axis_size('dp')), 'dp', 0, 0)]
    unnamed x19 -> x22, local copies, waits for them, and re-layouts: 15.3 us -> 13 us
  transfers between devices with their start and end apart: 7 -> 7, of which waited for: 5 -> 4; matrix products, arithmetic and copies ran while one was open for 3% -> 3% of each run, Pallas kernels for 0% -> 0%
where the time goes in v1:
time: 634 us
  waiting for transfers between devices  537 us (85%)
  matrix products  28.2 us (4%)
  starting transfers between devices  26.5 us (4%)
  local copies, waits for them, and re-layouts  22.8 us (4%)
  between operations  13.4 us (2%)
    all_gather x1, waiting for transfers between devices, on_device(): lax.all_gather(w_in, 'dp', axis=0, tiled=True)  163 us
    all_gather x1, waiting for transfers between devices, on_device(): lax.all_gather(w_key, 'dp', axis=0, tiled=True)  143 us
    all_gather x1, waiting for transfers between devices, on_device(): lax.all_gather(w_value, 'dp', axis=0, tiled=True)  141 us
    psum x1, waiting for transfers between devices, on_device(): total = lax.psum(partial_out, 'mp')  87.4 us
    all_to_all x1, starting transfers between devices, on_device(): lax.all_to_all(jnp.stack([w_out] * lax.axis_size('dp')), 'dp', 0, 0)  18.1 us
    dot_general x1, matrix products, on_device(): jnp.dot(hidden, jnp.concatenate(lax.all_to_all(jnp.stack([w_out] * lax.ax...  14.2 us
    unnamed x22, local copies, waits for them, and re-layouts  13 us
  transfers between devices with their start and end apart: 7, of which 4 were waited for; matrix products, arithmetic and copies ran while one was open for 3% of the time, Pallas kernels for 0%

profile of v1, /device:TPU:8, one launch (start us, length us, event | category | flops | bytes accessed | tf_op | source)
XLA Modules:
  0.0 633.5 jit_solution(12620977055046838769)
XLA Ops:
  6.5 2.3 stack.8
  8.9 18.1 %all-to-all-start.1 = ((bf16[32,896,28]{1,2,0:T(8,128)(2,1)}), bf16[32,896,28]{1,2,0:T(8,128)(2,1)}, u32[]{:S(2)}, u32[]{:S(2)}) async-start(bf16[32,896,28]{1,2,0:T(8,128)(2,1)} %stack.8), calls=%async_computation.1 | async-start | bytes 3670016 | tf_op jit(solution)/shard_map/all_to_all | solution.py:84
  28.2 1.7 fusion.5
  29.9 163.1 %all-gather.7.cloned.1.call-done = bf16[32,28,896]{2,1,0:T(8,128)(2,1)} async-done(((bf16[1,28,896]{2,1,0:T(8,128)(2,1)}), bf16[32,28,896]{2,1,0:T(8,128)(2,1)}) %all-gather.7.cloned.1.call-update) | async-done | bytes 1605648 | tf_op jit(solution)/shard_map/all_gather | solution.py:78
  193.0 2.4 reshape.115
  195.5 3.6 reshape.109
  199.1 14.2 %fusion.23 = f32[1024,896]{1,0:T(8,128)} fusion(bf16[896,896]{0,1:T(8,128)(2,1)} %reshape.109, bf16[1024,896]{1,0:T(8,128)(2,1)} %fusion.5, bf16[896,896]{1,0:T(8,128)(2,1)S(1)} %reshape.115), kind=kOutput, calls=%fused_computation.41 | convolution fusion | flops 3347972096 | bytes 8716288 | tf_op jit(solution)/shard_map/dot_general | solution.py:81
  215.7 3.2 all-to-all-start
  218.9 87.4 %all-reduce.2.cloned.1.call-done = f32[1024,896]{1,0:T(8,128)} async-done(((f32[1024,896]{1,0:T(8,128)}), f32[1024,896]{1,0:T(8,128)}) %all-reduce.2.cloned.1.call-update) | async-done | bytes 3670032 | tf_op jit(solution)/shard_map/psum | solution.py:88
  306.3 2.4 fusion.6
  308.7 2.8 convolution_convert_fusion
  311.5 2.4 copy.32
  314.0 5.1 all-to-all-start.2
  319.4 141.0 %all-gather.9.cloned.1.call-done = bf16[32,28,1024]{2,1,0:T(8,128)(2,1)} async-done(((bf16[1,28,1024]{2,1,0:T(8,128)(2,1)}), bf16[32,28,1024]{2,1,0:T(8,128)(2,1)}) %all-gather.9.cloned.1.call-update) | async-done | bytes 1835024 | tf_op jit(solution)/shard_map/all_gather | solution.py:103
  460.4 3.8 reshape.117
  464.2 143.3 %all-gather.11.cloned.1.call-done = bf16[32,28,1024]{2,1,0:T(8,128)(2,1)} async-done(((bf16[1,28,1024]{2,1,0:T(8,128)(2,1)}), bf16[32,28,1024]{2,1,0:T(8,128)(2,1)}) %all-gather.11.cloned.1.call-update) | async-done | bytes 1835024 | tf_op jit(solution)/shard_map/all_gather | solution.py:99
  607.5 3.7 reshape.119
  611.2 4.6 fusion.25
  616.0 2.3 convert_bitcast_fusion.1
  619.9 2.3 convert_bitcast_fusion
  622.9 0.9 bitcast_reduce_fusion
  623.8 0.9 fusion.28
  624.8 1.0 fusion.36
  626.1 0.9 copy.67
  (50 shorter events, 6.7 us)
Async XLA Ops:
  6.5 21.2 %copy-start = (bf16[4,256,896]{2,1,0:T(8,128)(2,1)S(1)}, bf16[4,256,896]{2,1,0:T(8,128)(2,1)}, u32[]{:S(2)}) copy-start(bf16[4,256,896]{2,1,0:T(8,128)(2,1)} %param.9) | copy-start | bytes 5505028
  6.5 21.6 %copy-start.4 = (f32[896]{0:T(1024)S(1)}, f32[896]{0:T(1024)}, u32[]{:S(2)}) copy-start(f32[896]{0:T(1024)} %param.12) | copy-start | bytes 10756
  8.9 186.6 %all-to-all-start.1 = ((bf16[32,896,28]{1,2,0:T(8,128)(2,1)}), bf16[32,896,28]{1,2,0:T(8,128)(2,1)}, u32[]{:S(2)}, u32[]{:S(2)}) async-start(bf16[32,896,28]{1,2,0:T(8,128)(2,1)} %stack.8), calls=%async_computation.1 | async-start | bytes 3670016 | tf_op jit(solution)/shard_map/all_to_all | solution.py:84
  26.9 166.1 %all-gather.7.cloned.1.call-start = ((), (), s32[]{:S(2)}) async-start(), calls=%async_computation.4 | async-start | bytes 1892352 | tf_op jit(solution)/shard_map/all_gather | solution.py:78
  27.7 278.7 %all-reduce.2.cloned.1.call-start = ((), (), s32[]{:S(2)}) async-start(), calls=%async_computation.3 | async-start | bytes 7340032 | tf_op jit(solution)/shard_map/psum | solution.py:88
  213.2 1.3 copy-start.6
  213.2 1.6 copy-start.5
  213.3 247.2 %all-gather.9.cloned.1.call-start = ((), (), s32[]{:S(2)}) async-start(), calls=%async_computation.5 | async-start | bytes 2162688 | tf_op jit(solution)/shard_map/all_gather | solution.py:103
  214.0 393.5 %all-gather.11.cloned.1.call-start = ((), (), s32[]{:S(2)}) async-start(), calls=%async_computation.6 | async-start | bytes 2162688 | tf_op jit(solution)/shard_map/all_gather | solution.py:99
  215.7 98.3 %all-to-all-start = ((s32[4,2,2]{1,2,0:T(2,128)}), s32[4,2,2]{1,2,0:T(2,128)S(1)}, u32[]{:S(2)}, u32[]{:S(2)}) async-start(s32[4,2,2]{1,2,0:T(2,128)} %copy.29), calls=%async_computation | async-start | bytes 8192 | tf_op jit(solution)/shard_map/all_to_all | solution.py:93
  314.0 5.1 copy-start.3
  314.0 297.2 %all-to-all-start.2 = ((bf16[8,256,896]{2,1,0:T(8,128)(2,1)}), bf16[8,256,896]{2,1,0:T(8,128)(2,1)}, u32[]{:S(2)}, u32[]{:S(2)}) async-start(bf16[8,256,896]{2,1,0:T(8,128)(2,1)} %copy.32), calls=%async_computation.2 | async-start | bytes 7340032 | tf_op jit(solution)/shard_map/all_to_all | solution.py:92
  611.2 4.8 copy-start.1
  618.4 1.5 copy-start.2
Sparse Core Ops, SparseCore 0:
  30.8 162.1 all-gather.6
  213.4 92.9 all-reduce.1
  309.4 150.9 all-gather.8
  463.4 144.0 all-gather.10
